TPU v7x, 32 devices: a whole 2x2x4 slice. The times are simulated.
32 devices in a mesh: seq: 4 (over y, x), col: 8 (over z, core).
Axes of the slice: x: 2, y: 2, z: 4, core: 2. Of those that a mesh axis runs over, the one named last changes fastest.
Arguments:
- alignment: bfloat16 [32, 128, 256], P('seq', 'col')
- row_query: bfloat16 [256, 128], replicated
- row_key: bfloat16 [256, 128], replicated
- row_value: bfloat16 [256, 128], replicated, may hold values from -0.375 to 0.375
- row_output: bfloat16 [128, 256], replicated, may hold values from -0.5 to 0.5
- column_query: bfloat16 [256, 128], replicated
- column_key: bfloat16 [256, 128], replicated
- column_value: bfloat16 [256, 128], replicated, may hold values from -0.375 to 0.375
- column_output: bfloat16 [128, 256], replicated, may hold values from -0.5 to 0.5
Outputs:
- row_update: bfloat16 [32, 128, 256], P('seq', 'col')
- layer_output: bfloat16 [32, 128, 256], P('seq', 'col')
All inputs are finite; a program needn't handle non-finite values.
Results may differ from a plain program's by a relative error of at most 0.014.
Values may be sent and summed in bfloat16 or wider, within the bound.
No kernel may reach another device: no remote copies, remote signals or barrier semaphores. Data moves between devices by JAX's collectives and lax.ppermute only.
A program may use at most 64 MiB of HBM per device.

v0:
```python
import jax
import jax.numpy as jnp
from jax import lax
from jax.sharding import PartitionSpec as P

HEADS = 4
HEAD_DIM = 32


def layer_norm(field):
    values = field.astype(jnp.float32)
    mean = jnp.mean(values, axis=-1, keepdims=True)
    centred = values - mean
    variance = jnp.mean(centred * centred, axis=-1, keepdims=True)
    return (centred * lax.rsqrt(variance + 1e-05)).astype(jnp.bfloat16)


def project(field, weight):
    return jnp.dot(field, weight, preferred_element_type=jnp.float32)


def column_attend(queries, keys, values):
    seq_rows, columns, inner = queries.shape
    query_heads = queries.reshape(seq_rows, columns, HEADS, HEAD_DIM)
    key_heads = keys.reshape(keys.shape[0], columns, HEADS, HEAD_DIM)
    value_heads = values.reshape(values.shape[0], columns, HEADS, HEAD_DIM)
    scores = jnp.einsum(
        "schd,tchd->chst", query_heads, key_heads, preferred_element_type=jnp.float32
    ) * float(HEAD_DIM) ** (-0.5)
    weights = jax.nn.softmax(scores, axis=-1).astype(jnp.bfloat16)
    context = jnp.einsum(
        "chst,tchd->schd", weights, value_heads, preferred_element_type=jnp.float32
    )
    return context.reshape(seq_rows, columns, inner).astype(jnp.bfloat16)


def on_device(
    alignment,
    row_query,
    row_key,
    row_value,
    row_output,
    column_query,
    column_key,
    column_value,
    column_output,
):
    seq_dev, col_dev, width = alignment.shape
    inner = row_query.shape[1]
    scale = float(HEAD_DIM * seq_dev * lax.axis_size("seq")) ** (-0.5)
    normed = layer_norm(alignment)
    queries = project(normed, row_query).astype(jnp.bfloat16)
    keys = project(normed, row_key).astype(jnp.bfloat16)
    values = project(normed, row_value).astype(jnp.bfloat16)
    query_heads = queries.reshape(seq_dev, col_dev, HEADS, HEAD_DIM)
    piece = lax.all_gather(keys, "col", axis=1, tiled=True)
    piece_heads = piece.reshape(seq_dev, piece.shape[1], HEADS, HEAD_DIM)
    partial_value = jnp.einsum(
        "sihd,sjhd->hij", query_heads, piece_heads, preferred_element_type=jnp.float32
    )
    logits = lax.psum(partial_value, "seq") * scale
    probs = jax.nn.softmax(logits, axis=-1).astype(jnp.bfloat16)
    piece = lax.all_gather(values, "col", axis=1, tiled=True)
    piece_heads = piece.reshape(seq_dev, piece.shape[1], HEADS, HEAD_DIM)
    context = jnp.einsum("hij,sjhd->sihd", probs, piece_heads, preferred_element_type=jnp.float32)
    context = context.reshape(seq_dev, col_dev, inner).astype(jnp.bfloat16)
    row_update = project(context, row_output).astype(jnp.bfloat16)
    middle = (alignment.astype(jnp.float32) + row_update.astype(jnp.float32)).astype(jnp.bfloat16)
    column_normed = layer_norm(middle)
    column_queries = project(column_normed, column_query).astype(jnp.bfloat16)
    column_keys = project(column_normed, column_key).astype(jnp.bfloat16)
    column_values = project(column_normed, column_value).astype(jnp.bfloat16)
    every_keys, every_values = (
        lax.all_gather(column_keys, "seq", axis=0, tiled=True),
        lax.all_gather(column_values, "seq", axis=0, tiled=True),
    )
    column_context = column_attend(column_queries, every_keys, every_values)
    layer_output = (middle.astype(jnp.float32) + project(column_context, column_output)).astype(
        jnp.bfloat16
    )
    return (row_update, layer_output)


def solution(mesh):
    return jax.shard_map(
        on_device,
        mesh=mesh,
        in_specs=(P("seq", "col", None), P(), P(), P(), P(), P(), P(), P(), P()),
        out_specs=(P("seq", "col", None), P("seq", "col", None)),
        check_vma=False,
    )
```

profile of v0, /device:TPU:0, one launch (start us, length us, event | category | flops | bytes accessed | tf_op | source)
XLA Modules:
  0.0 75.1 jit_solution(4044517943388862189)
XLA Ops:
  0.7 1.0 %convert_reduce_fusion.1 = f32[8,16]{1,0:T(8,128)S(1)} fusion(bf16[8,16,256]{2,1,0:T(8,128)(2,1)} %param.9), kind=kLoop, calls=%fused_computation.30 | loop fusion | flops 65408 | bytes 66048 | tf_op jit(solution)/shard_map/reduce_sum | solution.py:12
  1.7 0.2 fusion.19
  1.9 0.2 convolution_convert_fusion.6
  2.1 15.9 %all_gather.13 = bf16[8,128,128]{2,1,0:T(8,128)(2,1)S(1)} all-gather(bf16[8,16,128]{2,1,0:T(8,128)(2,1)S(1)} %convolution_convert_fusion.6), channel_id=1, replica_groups=mesh['seq'=4,'col'=8] {'col'}, dimensions={1}, use_global_device_ids=true | all-gather | bytes 294912 | tf_op jit(solution)/shard_map/all_gather | solution.py:56
  18.0 0.2 copy.36
  18.2 0.7 copy-done.4
  18.8 0.2 convolution_convert_fusion.7
  19.2 0.2 convolution_bitcast_fusion
  19.4 16.4 %psum.7 = f32[4,16,128]{2,1,0:T(8,128)S(1)} all-reduce(f32[4,16,128]{2,1,0:T(8,128)S(1)} %convolution_bitcast_fusion), channel_id=1, replica_groups=mesh['seq'=4,'col'=8] {'seq'}, use_global_device_ids=true, to_apply=%region_2.0 | all-reduce | flops 8192 | bytes 65536 | tf_op jit(solution)/shard_map/psum | solution.py:61
  35.9 0.2 fusion.51
  36.0 0.2 convolution_convert_fusion.8
  36.3 14.3 %all_gather.12 = bf16[8,128,128]{2,1,0:T(8,128)(2,1)S(1)} all-gather(bf16[8,16,128]{2,1,0:T(8,128)(2,1)S(1)} %convolution_convert_fusion.8), channel_id=1, replica_groups=mesh['seq'=4,'col'=8] {'col'}, dimensions={1}, use_global_device_ids=true | all-gather | bytes 294912 | tf_op jit(solution)/shard_map/all_gather | solution.py:63
  50.6 0.2 copy.35
  50.8 0.5 fusion.5
  51.2 0.1 copy.40
  51.5 0.8 %convert_reduce_fusion = (f32[8,16]{1,0:T(8,128)S(1)}, bf16[8,16,256]{2,1,0:T(8,128)(2,1)S(1)}, bf16[8,16,256]{2,1,0:T(8,128)(2,1)}) fusion(bf16[8,16,256]{2,1,0:T(8,128)(2,1)S(1)} %copy-done.1, bf16[8,16,128]{2,1,0:T(8,128)(2,1)S(1)} %convert_element_type.76, bf16[128,256]{1,0:T(8,128)(2,1)S(1)} %copy-done), kind=kOutput, calls=%fused_computation.27 | convolution fusion | flops 8617856 | bytes 295424 | tf_op jit(solution)/shard_map/dot_general | solution.py:19
  52.3 0.2 fusion.17
  52.5 0.6 copy-done.6
  53.1 0.2 convolution_convert_fusion.4
  53.5 0.7 copy-done.7
  54.2 0.2 convolution_convert_fusion.3
  54.4 7.5 %all_gather.15 = bf16[32,16,128]{2,1,0:T(8,128)(2,1)S(1)} all-gather(bf16[8,16,128]{2,1,0:T(8,128)(2,1)S(1)} %convolution_convert_fusion.3), channel_id=1, replica_groups=mesh['seq'=4,'col'=8] {'seq'}, dimensions={0}, use_global_device_ids=true | all-gather | bytes 163840 | tf_op jit(solution)/shard_map/all_gather | solution.py:74
  62.0 0.2 reshape.59
  62.2 0.5 convolution_multiply_fusion
  62.7 0.3 fusion.52
  63.0 0.6 copy-done.8
  63.5 0.2 convolution_convert_fusion.5
  63.8 8.4 %all_gather.14 = bf16[32,16,128]{2,1,0:T(8,128)(2,1)S(1)} all-gather(bf16[8,16,128]{2,1,0:T(8,128)(2,1)S(1)} %convolution_convert_fusion.5), channel_id=1, replica_groups=mesh['seq'=4,'col'=8] {'seq'}, dimensions={0}, use_global_device_ids=true | all-gather | bytes 163840 | tf_op jit(solution)/shard_map/all_gather | solution.py:75
  72.1 0.2 reshape.57
  72.4 1.0 %fusion.4 = bf16[8,16,4,32]{3,0,2,1:T(8,128)(2,1)S(1)} fusion(bf16[32,16,4,32]{3,2,1,0:T(4,128)(2,1)S(1)} %reshape.57, f32[16,4,8]{2,1,0:T(4,128)S(1)} %fusion.52, f32[16,4,8,32]{3,2,1,0:T(8,128)S(1)} %convolution_multiply_fusion), kind=kOutput, calls=%fused_computation.7 | convolution fusion | flops 1114655 | bytes 231424 | tf_op jit(solution)/shard_map/chst,tchd->schd/dot_general | solution.py:31
  73.6 0.7 copy-done.2
  74.3 0.8 %fusion.6 = bf16[8,16,256]{2,1,0:T(8,128)(2,1)} fusion(bf16[8,16,128]{2,1,0:T(8,128)(2,1)S(1)} %convert_element_type.88, bf16[8,16,256]{2,1,0:T(8,128)(2,1)S(1)} %get-tuple-element.3, bf16[128,256]{1,0:T(8,128)(2,1)S(1)} %copy-done.2), kind=kOutput, calls=%fused_computation.11 | convolution fusion | flops 8486912 | bytes 229376 | tf_op jit(solution)/shard_map/dot_general | solution.py:19
  (22 shorter events, 0.6 us)
Async XLA Ops:
  0.6 50.9 %copy-start = (bf16[128,256]{1,0:T(8,128)(2,1)S(1)}, bf16[128,256]{1,0:T(8,128)(2,1)}, u32[]{:S(2)}) copy-start(bf16[128,256]{1,0:T(8,128)(2,1)} %param.13) | copy-start | bytes 196612
  0.6 1.0 %copy-start.1 = (bf16[8,16,256]{2,1,0:T(8,128)(2,1)S(1)}, bf16[8,16,256]{2,1,0:T(8,128)(2,1)}, u32[]{:S(2)}) copy-start(bf16[8,16,256]{2,1,0:T(8,128)(2,1)} %param.9) | copy-start | bytes 196612
  0.7 1.2 %copy-start.3 = (bf16[256,128]{1,0:T(8,128)(2,1)S(1)}, bf16[256,128]{1,0:T(8,128)(2,1)}, u32[]{:S(2)}) copy-start(bf16[256,128]{1,0:T(8,128)(2,1)} %param.11) | copy-start | bytes 196612
  18.0 0.8 %copy-start.4 = (bf16[256,128]{1,0:T(8,128)(2,1)S(1)}, bf16[256,128]{1,0:T(8,128)(2,1)}, u32[]{:S(2)}) copy-start(bf16[256,128]{1,0:T(8,128)(2,1)} %param.10) | copy-start | bytes 196612
  19.4 16.6 %copy-start.5 = (bf16[256,128]{1,0:T(8,128)(2,1)S(1)}, bf16[256,128]{1,0:T(8,128)(2,1)}, u32[]{:S(2)}) copy-start(bf16[256,128]{1,0:T(8,128)(2,1)} %param.12) | copy-start | bytes 196612
  52.3 0.8 %copy-start.6 = (bf16[256,128]{1,0:T(8,128)(2,1)S(1)}, bf16[256,128]{1,0:T(8,128)(2,1)}, u32[]{:S(2)}) copy-start(bf16[256,128]{1,0:T(8,128)(2,1)} %param.14) | copy-start | bytes 196612
  53.4 0.8 %copy-start.7 = (bf16[256,128]{1,0:T(8,128)(2,1)S(1)}, bf16[256,128]{1,0:T(8,128)(2,1)}, u32[]{:S(2)}) copy-start(bf16[256,128]{1,0:T(8,128)(2,1)} %param.15) | copy-start | bytes 196612
  62.7 0.8 %copy-start.8 = (bf16[256,128]{1,0:T(8,128)(2,1)S(1)}, bf16[256,128]{1,0:T(8,128)(2,1)}, u32[]{:S(2)}) copy-start(bf16[256,128]{1,0:T(8,128)(2,1)} %param.16) | copy-start | bytes 196612
  73.4 0.8 %copy-start.2 = (bf16[128,256]{1,0:T(8,128)(2,1)S(1)}, bf16[128,256]{1,0:T(8,128)(2,1)}, u32[]{:S(2)}) copy-start(bf16[128,256]{1,0:T(8,128)(2,1)} %param.17) | copy-start | bytes 196612
where the time goes:
time: 75.6 us; the launch traced here: 75.1 us
  blocking collectives  62.6 us (83%)
  matrix products  5.07 us (7%)
  local copies, waits for them, and re-layouts  4.82 us (6%)
  other arithmetic  1.75 us (2%)
  between operations  0.86 us (1%)
    psum x1, blocking collectives, on_device(): logits = lax.psum(partial_value, 'seq') * scale  16.4 us
    all_gather x1, blocking collectives, on_device(): piece = lax.all_gather(keys, 'col', axis=1, tiled=True)  15.9 us
    all_gather x1, blocking collectives, on_device(): piece = lax.all_gather(values, 'col', axis=1, tiled=True)  14.3 us
    all_gather x1, blocking collectives, on_device(): lax.all_gather(column_values, 'seq', axis=0, tiled=True)  8.37 us
    all_gather x1, blocking collectives, on_device(): lax.all_gather(column_keys, 'seq', axis=0, tiled=True)  7.55 us
    unnamed x18, local copies, waits for them, and re-layouts  3.34 us
    dot_general x8, matrix products, project(): return jnp.dot(field, weight, preferred_element_type=jnp.float32)  2.87 us

commit v1 on v0

--- a/solution.py
+++ b/solution.py
@@ -1,3 +1,4 @@
+import functools
 import jax
 import jax.numpy as jnp
 from jax import lax
@@ -5,6 +6,24 @@
 
 HEADS = 4
 HEAD_DIM = 32
+
+
+def shapes_cut(row_data, ndim_at):
+    ledger = [row_data]
+    p = 0
+    cores_n = lax.axis_size("col")
+    while p < cores_n - 1:
+        part_now = lax.ppermute(ledger[-1], "col", [(h, (h + 1) % cores_n) for h in range(cores_n)])
+        ledger.append(part_now)
+        p = p + 1
+    current_value = jnp.concatenate(ledger[::-1], axis=ndim_at)
+    a_next = jnp.roll(
+        current_value, (lax.axis_index("col") + 1) * row_data.shape[ndim_at], axis=ndim_at
+    )
+    return a_next
+
+
+follow_streams = functools.partial(shapes_cut, ndim_at=1)
 
 
 def layer_norm(field):
@@ -60,7 +79,7 @@
     )
     logits = lax.psum(partial_value, "seq") * scale
     probs = jax.nn.softmax(logits, axis=-1).astype(jnp.bfloat16)
-    piece = lax.all_gather(values, "col", axis=1, tiled=True)
+    piece = follow_streams(values)
     piece_heads = piece.reshape(seq_dev, piece.shape[1], HEADS, HEAD_DIM)
     context = jnp.einsum("hij,sjhd->sihd", probs, piece_heads, preferred_element_type=jnp.float32)
     context = context.reshape(seq_dev, col_dev, inner).astype(jnp.bfloat16)

time: 75.6 us -> 86.3 us (1.14)
  waiting for transfers between devices: 0 us -> 25.5 us
  blocking collectives: 62.6 us -> 47.2 us
  starting transfers between devices: 0 us -> 1.01 us
    ppermute x0 -> x7, waiting for transfers between devices: none -> 25.5 us  [shapes_cut(): lax.ppermute(ledger[-1], 'col', [(h, (h + 1) % cores_n) for h in range(co...]
    all_gather x1 -> x0, blocking collectives: 14.3 us -> none  [on_device(): piece = lax.all_gather(values, 'col', axis=1, tiled=True)]
    all_gather x1, blocking collectives: 15.9 us -> 14.3 us  [on_device(): piece = lax.all_gather(keys, 'col', axis=1, tiled=True)]
    ppermute x0 -> x7, starting transfers between devices: none -> 1.01 us  [shapes_cut(): lax.ppermute(ledger[-1], 'col', [(h, (h + 1) % cores_n) for h in range(co...]
    unnamed x18 -> x33, local copies, waits for them, and re-layouts: 3.34 us -> 2.84 us
  transfers between devices with their start and end apart: 0 -> 7, of which waited for: 0 -> 5; matrix products, arithmetic and copies ran while one was open for 0% -> 1% of each run, Pallas kernels for 0% -> 0%
where the time goes in v1:
time: 86.3 us; the launch traced here: 85.9 us
  blocking collectives  47.2 us (55%)
  waiting for transfers between devices  25.5 us (30%)
  matrix products  5.06 us (6%)
  local copies, waits for them, and re-layouts  4.36 us (5%)
  other arithmetic  1.75 us (2%)
  starting transfers between devices  1.01 us (1%)
  between operations  0.98 us (1%)
    ppermute x7, waiting for transfers between devices, shapes_cut(): lax.ppermute(ledger[-1], 'col', [(h, (h + 1) % cores_n) for h in range(co...  25.5 us
    psum x1, blocking collectives, on_device(): logits = lax.psum(partial_value, 'seq') * scale  16.8 us
    all_gather x1, blocking collectives, on_device(): piece = lax.all_gather(keys, 'col', axis=1, tiled=True)  14.3 us
    all_gather x1, blocking collectives, on_device(): lax.all_gather(column_values, 'seq', axis=0, tiled=True)  8.38 us
    all_gather x1, blocking collectives, on_device(): lax.all_gather(column_keys, 'seq', axis=0, tiled=True)  7.71 us
    dot_general x8, matrix products, project(): return jnp.dot(field, weight, preferred_element_type=jnp.float32)  2.86 us
    unnamed x33, local copies, waits for them, and re-layouts  2.84 us
  transfers between devices with their start and end apart: 7, of which 5 were waited for; matrix products, arithmetic and copies ran while one was open for 1% of the time, Pallas kernels for 0%

profile of v1, /device:TPU:0, one launch (start us, length us, event | category | flops | bytes accessed | tf_op | source)
XLA Modules:
  0.0 85.9 jit_solution(8940645771085927193)
XLA Ops:
  0.7 1.0 %convert_reduce_fusion.1 = f32[8,16]{1,0:T(8,128)S(1)} fusion(bf16[8,16,256]{2,1,0:T(8,128)(2,1)} %param.9), kind=kLoop, calls=%fused_computation.30 | loop fusion | flops 65408 | bytes 66048 | tf_op jit(solution)/shard_map/reduce_sum | solution.py:31
  1.9 0.2 convolution_convert_fusion.8
  2.1 0.5 collective-permute-start
  2.7 5.6 %collective-permute-done = bf16[8,16,128]{2,1,0:T(8,128)(2,1)S(1)} collective-permute-done((bf16[8,16,128]{2,1,0:T(8,128)(2,1)S(1)}, bf16[8,16,128]{2,1,0:T(8,128)(2,1)S(1)}, u32[]{:S(2)}, u32[]{:S(2)}) %collective-permute-start) | collective-permute-done | bytes 32800 | tf_op jit(solution)/shard_map/ppermute | solution.py:16
  8.3 5.1 %collective-permute-done.1 = bf16[8,16,128]{2,1,0:T(8,128)(2,1)S(1)} collective-permute-done((bf16[8,16,128]{2,1,0:T(8,128)(2,1)S(1)}, bf16[8,16,128]{2,1,0:T(8,128)(2,1)S(1)}, u32[]{:S(2)}, u32[]{:S(2)}) %collective-permute-start.1) | collective-permute-done | bytes 32800 | tf_op jit(solution)/shard_map/ppermute | solution.py:16
  13.4 0.2 convolution_convert_fusion.6
  13.7 4.9 %collective-permute-done.2 = bf16[8,16,128]{2,1,0:T(8,128)(2,1)S(1)} collective-permute-done((bf16[8,16,128]{2,1,0:T(8,128)(2,1)S(1)}, bf16[8,16,128]{2,1,0:T(8,128)(2,1)S(1)}, u32[]{:S(2)}, u32[]{:S(2)}) %collective-permute-start.2) | collective-permute-done | bytes 32800 | tf_op jit(solution)/shard_map/ppermute | solution.py:16
  18.6 0.2 convolution_convert_fusion.7
  18.8 4.9 %collective-permute-done.3 = bf16[8,16,128]{2,1,0:T(8,128)(2,1)S(1)} collective-permute-done((bf16[8,16,128]{2,1,0:T(8,128)(2,1)S(1)}, bf16[8,16,128]{2,1,0:T(8,128)(2,1)S(1)}, u32[]{:S(2)}, u32[]{:S(2)}) %collective-permute-start.3) | collective-permute-done | bytes 32800 | tf_op jit(solution)/shard_map/ppermute | solution.py:16
  23.7 14.3 %all_gather.9 = bf16[8,128,128]{2,1,0:T(8,128)(2,1)S(1)} all-gather(bf16[8,16,128]{2,1,0:T(8,128)(2,1)S(1)} %convolution_convert_fusion.6), channel_id=1, replica_groups=mesh['seq'=4,'col'=8] {'col'}, dimensions={1}, use_global_device_ids=true | all-gather | bytes 294912 | tf_op jit(solution)/shard_map/all_gather | solution.py:75
  38.3 0.4 collective-permute-start.5
  38.7 0.2 convolution_bitcast_fusion
  38.9 16.8 %psum.7 = f32[4,16,128]{2,1,0:T(8,128)S(1)} all-reduce(f32[4,16,128]{2,1,0:T(8,128)S(1)} %convolution_bitcast_fusion), channel_id=1, replica_groups=mesh['seq'=4,'col'=8] {'seq'}, use_global_device_ids=true, to_apply=%region_2.0 | all-reduce | flops 8192 | bytes 65536 | tf_op jit(solution)/shard_map/psum | solution.py:80
  56.0 5.0 %collective-permute-done.6 = bf16[8,16,128]{2,1,0:T(8,128)(2,1)S(1)} collective-permute-done((bf16[8,16,128]{2,1,0:T(8,128)(2,1)S(1)}, bf16[8,16,128]{2,1,0:T(8,128)(2,1)S(1)}, u32[]{:S(2)}, u32[]{:S(2)}) %collective-permute-start.6) | collective-permute-done | bytes 32800 | tf_op jit(solution)/shard_map/ppermute | solution.py:16
  61.2 0.2 copy.34
  61.4 0.5 fusion.5
  62.1 0.8 convert_reduce_fusion
  63.1 0.6 copy-done.6
  63.8 0.2 convolution_convert_fusion.4
  64.1 0.7 copy-done.7
  64.8 0.2 convolution_convert_fusion.3
  65.1 7.7 %all_gather.11 = bf16[32,16,128]{2,1,0:T(8,128)(2,1)S(1)} all-gather(bf16[8,16,128]{2,1,0:T(8,128)(2,1)S(1)} %convolution_convert_fusion.3), channel_id=1, replica_groups=mesh['seq'=4,'col'=8] {'seq'}, dimensions={0}, use_global_device_ids=true | all-gather | bytes 163840 | tf_op jit(solution)/shard_map/all_gather | solution.py:93
  72.8 0.2 reshape.59
  73.0 0.5 convolution_multiply_fusion
  73.5 0.3 fusion.52
  73.8 0.6 copy-done.8
  74.3 0.2 convolution_convert_fusion.5
  74.6 8.4 %all_gather.10 = bf16[32,16,128]{2,1,0:T(8,128)(2,1)S(1)} all-gather(bf16[8,16,128]{2,1,0:T(8,128)(2,1)S(1)} %convolution_convert_fusion.5), channel_id=1, replica_groups=mesh['seq'=4,'col'=8] {'seq'}, dimensions={0}, use_global_device_ids=true | all-gather | bytes 163840 | tf_op jit(solution)/shard_map/all_gather | solution.py:94
  82.9 0.2 reshape.57
  83.2 1.0 %fusion.4 = bf16[8,16,4,32]{3,0,2,1:T(8,128)(2,1)S(1)} fusion(bf16[32,16,4,32]{3,2,1,0:T(4,128)(2,1)S(1)} %reshape.57, f32[16,4,8]{2,1,0:T(4,128)S(1)} %fusion.52, f32[16,4,8,32]{3,2,1,0:T(8,128)S(1)} %convolution_multiply_fusion), kind=kOutput, calls=%fused_computation.7 | convolution fusion | flops 1114655 | bytes 231424 | tf_op jit(solution)/shard_map/chst,tchd->schd/dot_general | solution.py:50
  84.4 0.7 copy-done.2
  85.1 0.8 fusion.6
  (52 shorter events, 1.6 us)
Async XLA Ops:
  0.6 61.5 %copy-start = (bf16[128,256]{1,0:T(8,128)(2,1)S(1)}, bf16[128,256]{1,0:T(8,128)(2,1)}, u32[]{:S(2)}) copy-start(bf16[128,256]{1,0:T(8,128)(2,1)} %param.13) | copy-start | bytes 196612
  0.6 1.0 %copy-start.1 = (bf16[8,16,256]{2,1,0:T(8,128)(2,1)S(1)}, bf16[8,16,256]{2,1,0:T(8,128)(2,1)}, u32[]{:S(2)}) copy-start(bf16[8,16,256]{2,1,0:T(8,128)(2,1)} %param.9) | copy-start | bytes 196612
  0.7 1.2 %copy-start.3 = (bf16[256,128]{1,0:T(8,128)(2,1)S(1)}, bf16[256,128]{1,0:T(8,128)(2,1)}, u32[]{:S(2)}) copy-start(bf16[256,128]{1,0:T(8,128)(2,1)} %param.12) | copy-start | bytes 196612
  1.9 11.6 %copy-start.4 = (bf16[256,128]{1,0:T(8,128)(2,1)S(1)}, bf16[256,128]{1,0:T(8,128)(2,1)}, u32[]{:S(2)}) copy-start(bf16[256,128]{1,0:T(8,128)(2,1)} %param.11) | copy-start | bytes 196612
  2.1 16.5 %copy-start.5 = (bf16[256,128]{1,0:T(8,128)(2,1)S(1)}, bf16[256,128]{1,0:T(8,128)(2,1)}, u32[]{:S(2)}) copy-start(bf16[256,128]{1,0:T(8,128)(2,1)} %param.10) | copy-start | bytes 196612
  2.1 6.2 %collective-permute-start = (bf16[8,16,128]{2,1,0:T(8,128)(2,1)S(1)}, bf16[8,16,128]{2,1,0:T(8,128)(2,1)S(1)}, u32[]{:S(2)}, u32[]{:S(2)}) collective-permute-start(bf16[8,16,128]{2,1,0:T(8,128)(2,1)S(1)} %convolution_convert_fusion.8), channel_id=1, source_target_pairs={{0,1},{1,2},{2,3},{3,4},{4,5},{5,6},{6,7},{7,0},{8,9},{9,10},{10,1... | collective-permute-start | bytes 98312 | tf_op jit(solution)/shard_map/ppermute | solution.py:16
  8.3 5.1 %collective-permute-start.1 = (bf16[8,16,128]{2,1,0:T(8,128)(2,1)S(1)}, bf16[8,16,128]{2,1,0:T(8,128)(2,1)S(1)}, u32[]{:S(2)}, u32[]{:S(2)}) collective-permute-start(bf16[8,16,128]{2,1,0:T(8,128)(2,1)S(1)} %collective-permute-done), channel_id=1, source_target_pairs={{0,1},{1,2},{2,3},{3,4},{4,5},{5,6},{6,7},{7,0},{8,9},{9,10},{10,1... | collective-permute-start | bytes 98312 | tf_op jit(solution)/shard_map/ppermute | solution.py:16
  13.4 5.1 %collective-permute-start.2 = (bf16[8,16,128]{2,1,0:T(8,128)(2,1)S(1)}, bf16[8,16,128]{2,1,0:T(8,128)(2,1)S(1)}, u32[]{:S(2)}, u32[]{:S(2)}) collective-permute-start(bf16[8,16,128]{2,1,0:T(8,128)(2,1)S(1)} %collective-permute-done.1), channel_id=1, source_target_pairs={{0,1},{1,2},{2,3},{3,4},{4,5},{5,6},{6,7},{7,0},{8,9},{9,10},{10,1... | collective-permute-start | bytes 98312 | tf_op jit(solution)/shard_map/ppermute | solution.py:16
  18.6 5.1 %collective-permute-start.3 = (bf16[8,16,128]{2,1,0:T(8,128)(2,1)S(1)}, bf16[8,16,128]{2,1,0:T(8,128)(2,1)S(1)}, u32[]{:S(2)}, u32[]{:S(2)}) collective-permute-start(bf16[8,16,128]{2,1,0:T(8,128)(2,1)S(1)} %collective-permute-done.2), channel_id=1, source_target_pairs={{0,1},{1,2},{2,3},{3,4},{4,5},{5,6},{6,7},{7,0},{8,9},{9,10},{10,1... | collective-permute-start | bytes 98312 | tf_op jit(solution)/shard_map/ppermute | solution.py:16
  23.7 14.6 %collective-permute-start.4 = (bf16[8,16,128]{2,1,0:T(8,128)(2,1)S(1)}, bf16[8,16,128]{2,1,0:T(8,128)(2,1)S(1)}, u32[]{:S(2)}, u32[]{:S(2)}) collective-permute-start(bf16[8,16,128]{2,1,0:T(8,128)(2,1)S(1)} %collective-permute-done.3), channel_id=1, source_target_pairs={{0,1},{1,2},{2,3},{3,4},{4,5},{5,6},{6,7},{7,0},{8,9},{9,10},{10,1... | collective-permute-start | bytes 98312 | tf_op jit(solution)/shard_map/ppermute | solution.py:16
  38.3 17.4 %collective-permute-start.5 = (bf16[8,16,128]{2,1,0:T(8,128)(2,1)S(1)}, bf16[8,16,128]{2,1,0:T(8,128)(2,1)S(1)}, u32[]{:S(2)}, u32[]{:S(2)}) collective-permute-start(bf16[8,16,128]{2,1,0:T(8,128)(2,1)S(1)} %collective-permute-done.4), channel_id=1, source_target_pairs={{0,1},{1,2},{2,3},{3,4},{4,5},{5,6},{6,7},{7,0},{8,9},{9,10},{10,1... | collective-permute-start | bytes 98312 | tf_op jit(solution)/shard_map/ppermute | solution.py:16
  55.8 5.2 %collective-permute-start.6 = (bf16[8,16,128]{2,1,0:T(8,128)(2,1)S(1)}, bf16[8,16,128]{2,1,0:T(8,128)(2,1)S(1)}, u32[]{:S(2)}, u32[]{:S(2)}) collective-permute-start(bf16[8,16,128]{2,1,0:T(8,128)(2,1)S(1)} %collective-permute-done.5), channel_id=1, source_target_pairs={{0,1},{1,2},{2,3},{3,4},{4,5},{5,6},{6,7},{7,0},{8,9},{9,10},{10,1... | collective-permute-start | bytes 98312 | tf_op jit(solution)/shard_map/ppermute | solution.py:16
  62.9 0.8 copy-start.6
  64.0 0.8 copy-start.7
  73.5 0.8 copy-start.8
  84.3 0.8 copy-start.2
